TPU v7x, 768 devices: a whole 4x8x12 slice. The times are simulated.
768 devices in a mesh: seq: 48 (over y_lo, z, core), fsdp: 16 (over y_hi, x).
Axes of the slice: x: 4, y: 8 (y_hi: 4, y_lo: 2; y = y_hi * 2 + y_lo), z: 12, core: 2. Of those that a mesh axis runs over, the one named last changes fastest.
Arguments:
- queries: bfloat16 [16, 6144, 1024], P('fsdp', 'seq'), may hold values from -6 to 6
- keys: bfloat16 [16, 6144, 1024], P('fsdp', 'seq'), may hold values from -6 to 6
- values: bfloat16 [16, 6144, 1024], P('fsdp', 'seq'), may hold values from -6 to 6
- d_out: bfloat16 [16, 6144, 2048], P('fsdp', 'seq'), may hold values from -6 to 6
- w_out: bfloat16 [1024, 2048], P('fsdp'), may hold values from -0.1875 to 0.1875
- pattern: int32 [48, 4], replicated, may hold values from 0 to 47, as said below
- valid: int32 [16, 48], P('fsdp'), may hold values from 2 to 128, as said below
Outputs:
- d_queries: bfloat16 [16, 6144, 1024], P('fsdp', 'seq')
- d_keys: bfloat16 [16, 6144, 1024], P('fsdp', 'seq')
- d_values: bfloat16 [16, 6144, 1024], P('fsdp', 'seq')
Inputs may be any that keep to these rules, and one draw needn't show every extreme that they name: Row b of the pattern, for a query block of shard p, lists the first block of shard p, block b itself, one block of shard p - 1 and one block of shard p + 1; at the first and last shard the missing neighbour's entry repeats the first block of shard p. A block listed twice is attended once. The valid patches of a shard are its first ones; every sample has a shard whose 128 patches are all valid.
All inputs are finite; a program needn't handle non-finite values.
Results may differ from a plain program's by a relative error of at most 0.018.
Values may be sent and summed in bfloat16 or wider, within the bound.
A program may use at most 32 MiB of HBM per device.

v0:
```python
import jax
import jax.numpy as jnp
from jax import lax
from jax.sharding import PartitionSpec as P

HEADS = 8
HD = 128
BLOCK = 128
BLK_DEV = 1


def with_halo(cells, sides, width):
    for axis, dim in sides:
        count = lax.axis_size(axis)
        ends = count - 1
        head = lax.slice_in_dim(cells, 0, width, axis=dim)
        tail = lax.slice_in_dim(cells, cells.shape[dim] - width, cells.shape[dim], axis=dim)
        cells = jnp.concatenate(
            [
                lax.ppermute(tail, axis, [(i, (i + 1) % count) for i in range(ends)]),
                cells,
                lax.ppermute(head, axis, [((i + 1) % count, i) for i in range(ends)]),
            ],
            axis=dim,
        )
    return cells


def head_split(rows):
    return rows.reshape(rows.shape[0], HEADS, HD)


def allowed_mask(pattern, valid_row, query_shard, key_shard, query_span, key_span, pad_value):
    per_shard = BLK_DEV * BLOCK
    padded = jnp.pad(pattern, ((BLK_DEV, BLK_DEV), (0, 0)), constant_values=pad_value)
    listed_rows = lax.dynamic_slice_in_dim(
        padded, (query_shard + 1) * BLK_DEV, query_span * BLK_DEV, 0
    )
    key_blocks = key_shard * BLK_DEV + jnp.arange(key_span * BLK_DEV, dtype=jnp.int32)
    listed = jnp.any(listed_rows[:, :, None] == key_blocks[None, None, :], axis=1)
    key_pos = jnp.arange(key_span * per_shard, dtype=jnp.int32)
    owner = key_shard + key_pos // per_shard
    shards = jnp.arange(valid_row.shape[0], dtype=jnp.int32)
    owner_count = jnp.sum(
        jnp.where(owner[:, None] == shards[None, :], valid_row[None, :], 0), axis=1
    )
    key_ok = key_pos % per_shard < owner_count
    rows_q = query_span * BLK_DEV
    rows_k = key_span * BLK_DEV
    spread = jnp.broadcast_to(listed[:, None, :, None], (rows_q, BLOCK, rows_k, BLOCK))
    return spread.reshape(rows_q * BLOCK, rows_k * BLOCK) & key_ok[None, :]


def body(queries, keys, values, d_out, w_out, pattern, valid):
    shard = lax.axis_index("seq")
    tok = queries.shape[1]
    width = queries.shape[2]
    valid_row = valid[0]
    pad_value = -(pattern.shape[0] + BLK_DEV + 1)
    scale = HD ** (-0.5)
    cotangent_rows = d_out[0]
    d_attn = jnp.einsum(
        "td,rd->tr",
        cotangent_rows,
        lax.all_gather(w_out, "fsdp", axis=0, tiled=True),
        preferred_element_type=jnp.float32,
    ).astype(jnp.bfloat16)
    band_keys, band_values = (
        with_halo(keys, (("seq", 1),), tok),
        with_halo(values, (("seq", 1),), tok),
    )
    q_heads = head_split(queries[0])
    d_heads = head_split(d_attn)
    k_heads = head_split(band_keys[0])
    v_heads = head_split(band_values[0])
    mask = allowed_mask(pattern, valid_row, shard, shard - 1, 1, 3, pad_value)
    score = jnp.einsum("qhd,khd->hqk", q_heads, k_heads, preferred_element_type=jnp.float32) * scale
    score = jnp.where(mask[None], score, -jnp.inf)
    top = jnp.max(score, axis=2, keepdims=True)
    lse = top + jnp.log(jnp.sum(jnp.exp(score - top), axis=2, keepdims=True))
    prob = jnp.exp(score - lse)
    prob_b = prob.astype(jnp.bfloat16)
    out_rows = jnp.einsum("hqk,khd->hqd", prob_b, v_heads, preferred_element_type=jnp.float32)
    delta = jnp.sum(jnp.transpose(d_heads, (1, 0, 2)) * out_rows, axis=2, keepdims=True)
    d_prob = jnp.einsum("qhd,khd->hqk", d_heads, v_heads, preferred_element_type=jnp.float32)
    d_score = (prob * (d_prob - delta)).astype(jnp.bfloat16)
    d_query = (
        jnp.einsum("hqk,khd->qhd", d_score, k_heads, preferred_element_type=jnp.float32) * scale
    )
    d_query = d_query.reshape(tok, width).astype(jnp.bfloat16)[None]
    lse_rows = jnp.transpose(lse[:, :, 0])[None]
    delta_rows = jnp.transpose(delta[:, :, 0])[None]
    band_queries, band_cotangent = (
        with_halo(queries, (("seq", 1),), tok),
        with_halo(d_attn[None], (("seq", 1),), tok),
    )
    band_lse, band_delta = (
        with_halo(lse_rows, (("seq", 1),), tok),
        with_halo(delta_rows, (("seq", 1),), tok),
    )
    far_q = head_split(band_queries[0])
    far_d = head_split(band_cotangent[0])
    own_k = head_split(keys[0])
    own_v = head_split(values[0])
    mask_keys = allowed_mask(pattern, valid_row, shard - 1, shard, 3, 1, pad_value)
    score_keys = (
        jnp.einsum("qhd,khd->hqk", far_q, own_k, preferred_element_type=jnp.float32) * scale
    )
    score_keys = jnp.where(mask_keys[None], score_keys, -jnp.inf)
    prob_keys = jnp.exp(score_keys - jnp.transpose(band_lse[0])[:, :, None])
    prob_keys_b = prob_keys.astype(jnp.bfloat16)
    d_prob_keys = jnp.einsum("qhd,khd->hqk", far_d, own_v, preferred_element_type=jnp.float32)
    d_score_keys = (prob_keys * (d_prob_keys - jnp.transpose(band_delta[0])[:, :, None])).astype(
        jnp.bfloat16
    )
    key_grad = (
        jnp.einsum("hqk,qhd->khd", d_score_keys, far_q, preferred_element_type=jnp.float32) * scale
    )
    value_grad = jnp.einsum("hqk,qhd->khd", prob_keys_b, far_d, preferred_element_type=jnp.float32)
    key_grad = key_grad.reshape(tok, width)
    value_grad = value_grad.reshape(tok, width)
    return (d_query, key_grad.astype(jnp.bfloat16)[None], value_grad.astype(jnp.bfloat16)[None])


def solution(mesh):
    in_specs = (
        P("fsdp", "seq", None),
        P("fsdp", "seq", None),
        P("fsdp", "seq", None),
        P("fsdp", "seq", None),
        P("fsdp", None),
        P(),
        P("fsdp", None),
    )
    out_specs = (P("fsdp", "seq", None), P("fsdp", "seq", None), P("fsdp", "seq", None))
    return jax.shard_map(body, mesh=mesh, in_specs=in_specs, out_specs=out_specs, check_vma=False)
```

profile of v0, /device:TPU:56, one launch (start us, length us, event | category | flops | bytes accessed | tf_op | source)
XLA Modules:
  0.0 151.0 jit_solution(15485739680073886357)
XLA Ops:
  7.3 0.7 all-gather.2.cloned.1.call-update
  8.0 1.1 copy.73
  9.1 14.8 %collective-permute-start.3 = (bf16[1,128,1024]{1,2,0:T(8,128)(2,1)S(1)}, bf16[1,128,1024]{1,2,0:T(8,128)(2,1)}, u32[]{:S(2)}, u32[]{:S(2)}) collective-permute-start(bf16[1,128,1024]{1,2,0:T(8,128)(2,1)S(1)} %copy.73), channel_id=1, source_target_pairs={{16,0},{32,16},{48,32},{64,48},{80,64},{96,80},{112,96},{128,112},... | collective-permute-start | bytes 786440 | tf_op jit(solution)/shard_map/ppermute | solution.py:22
  23.9 1.9 %collective-permute-start.2 = (bf16[1,128,1024]{1,2,0:T(8,128)(2,1)S(1)}, bf16[1,128,1024]{1,2,0:T(8,128)(2,1)}, u32[]{:S(2)}, u32[]{:S(2)}) collective-permute-start(bf16[1,128,1024]{1,2,0:T(8,128)(2,1)S(1)} %copy.73), channel_id=1, source_target_pairs={{0,16},{16,32},{32,48},{48,64},{64,80},{80,96},{96,112},{112,128},... | collective-permute-start | bytes 786440 | tf_op jit(solution)/shard_map/ppermute | solution.py:20
  25.8 1.1 copy.68
  27.0 5.8 %collective-permute-start.1 = (bf16[1,128,1024]{1,2,0:T(8,128)(2,1)S(1)}, bf16[1,128,1024]{1,2,0:T(8,128)(2,1)S(1)}, u32[]{:S(2)}, u32[]{:S(2)}) collective-permute-start(bf16[1,128,1024]{1,2,0:T(8,128)(2,1)S(1)} %copy.68), channel_id=1, source_target_pairs={{16,0},{32,16},{48,32},{64,48},{80,64},{96,80},{112,96},{128,112},... | collective-permute-start | bytes 786440 | tf_op jit(solution)/shard_map/ppermute | solution.py:22
  32.7 1.9 %collective-permute-start = (bf16[1,128,1024]{1,2,0:T(8,128)(2,1)S(1)}, bf16[1,128,1024]{1,2,0:T(8,128)(2,1)S(1)}, u32[]{:S(2)}, u32[]{:S(2)}) collective-permute-start(bf16[1,128,1024]{1,2,0:T(8,128)(2,1)S(1)} %copy.68), channel_id=1, source_target_pairs={{0,16},{16,32},{32,48},{48,64},{64,80},{80,96},{96,112},{112,128},... | collective-permute-start | bytes 786440 | tf_op jit(solution)/shard_map/ppermute | solution.py:20
  34.7 1.1 copy.82
  35.8 5.7 %collective-permute-start.5 = (bf16[1,128,1024]{1,2,0:T(8,128)(2,1)S(1)}, bf16[1,128,1024]{1,2,0:T(8,128)(2,1)}, u32[]{:S(2)}, u32[]{:S(2)}) collective-permute-start(bf16[1,128,1024]{1,2,0:T(8,128)(2,1)S(1)} %copy.82), channel_id=1, source_target_pairs={{16,0},{32,16},{48,32},{64,48},{80,64},{96,80},{112,96},{128,112},... | collective-permute-start | bytes 786440 | tf_op jit(solution)/shard_map/ppermute | solution.py:22
  41.6 0.2 dynamic-slice_reduce_fusion
  41.8 0.1 fusion.45
  41.9 0.1 select_reduce_fusion.1
  42.0 0.1 compare_reduce_fusion
  42.1 0.1 select_reduce_fusion
  42.2 0.1 bitcast_and_fusion
  42.3 0.8 copy.108
  43.2 0.1 broadcast_and_fusion
  43.3 1.9 %collective-permute-start.4 = (bf16[1,128,1024]{1,2,0:T(8,128)(2,1)S(1)}, bf16[1,128,1024]{1,2,0:T(8,128)(2,1)S(1)}, u32[]{:S(2)}, u32[]{:S(2)}) collective-permute-start(bf16[1,128,1024]{1,2,0:T(8,128)(2,1)S(1)} %copy.82), channel_id=1, source_target_pairs={{0,16},{16,32},{32,48},{48,64},{64,80},{80,96},{96,112},{112,128},... | collective-permute-start | bytes 786440 | tf_op jit(solution)/shard_map/ppermute | solution.py:20
  45.3 0.1 pad_maximum_fusion
  45.4 0.5 bitcast_reduce_fusion
  45.9 0.2 fusion.1
  46.1 5.8 %collective-permute-start.7 = (f32[1,128,8]{1,2,0:T(8,128)S(1)}, f32[1,128,8]{1,2,0:T(8,128)S(1)}, u32[]{:S(2)}, u32[]{:S(2)}) collective-permute-start(f32[1,128,8]{1,2,0:T(8,128)S(1)} %bitcast.117), channel_id=1, source_target_pairs={{16,0},{32,16},{48,32},{64,48},{80,64},{96,80},{112,96},{128,112},... | collective-permute-start | bytes 12296 | tf_op jit(solution)/shard_map/ppermute | solution.py:22
  51.9 1.9 %collective-permute-start.6 = (f32[1,128,8]{1,2,0:T(8,128)S(1)}, f32[1,128,8]{1,2,0:T(8,128)S(1)}, u32[]{:S(2)}, u32[]{:S(2)}) collective-permute-start(f32[1,128,8]{1,2,0:T(8,128)S(1)} %bitcast.118), channel_id=1, source_target_pairs={{0,16},{16,32},{32,48},{48,64},{64,80},{80,96},{96,112},{112,128},... | collective-permute-start | bytes 12296 | tf_op jit(solution)/shard_map/ppermute | solution.py:20
  53.8 1.1 pad_maximum_fusion.2
  54.9 1.6 %fusion.33 = f32[8,384,128]{2,1,0:T(8,128)} fusion(bf16[384,8,128]{0,2,1:T(8,128)(2,1)S(1)} %bitcast.103, bf16[128,8,128]{2,1,0:T(8,128)(2,1)S(1)} %bitcast.106), kind=kOutput, calls=%fused_computation.43 | convolution fusion | flops 100663296 | bytes 2621440 | tf_op jit(solution)/shard_map/qhd,khd->hqk/dot_general | solution.py:107
  56.5 2.0 %pad_maximum_fusion.1 = bf16[1,384,1024]{1,2,0:T(8,128)(2,1)} fusion(bf16[1,128,1024]{1,2,0:T(8,128)(2,1)} %collective-permute-done.3, bf16[1,128,1024]{1,2,0:T(8,128)(2,1)S(1)} %copy.73, bf16[1,128,1024]{1,2,0:T(8,128)(2,1)} %collective-permute-done.2), kind=kLoop, calls=%fused_computation.22 | loop fusion | flops 2359296 | bytes 1572864 | tf_op jit(solution)/shard_map/concatenate | solution.py:18
  58.6 0.3 collective-permute-done.6
  58.9 45.5 %all-gather.2.cloned.1.call-done = bf16[1024,2048]{1,0:T(8,128)(2,1)} async-done(((bf16[64,2048]{1,0:T(8,128)(2,1)}), bf16[1024,2048]{1,0:T(8,128)(2,1)}) %all-gather.2.cloned.1.call-update) | async-done | bytes 4194320 | tf_op jit(solution)/shard_map/all_gather | solution.py:65
  104.4 3.7 %convolution_convert_fusion.1 = bf16[128,1024]{1,0:T(8,128)(2,1)S(1)} fusion(bf16[1024,2048]{1,0:T(8,128)(2,1)} %all-gather.2.cloned.1.call-done, bf16[1,128,2048]{2,1,0:T(8,128)(2,1)S(1)} %copy-done), kind=kOutput, calls=%fused_computation.18 | convolution fusion | flops 537001984 | bytes 4980736 | tf_op jit(solution)/shard_map/td,rd->tr/dot_general | solution.py:62
  108.1 7.4 %collective-permute-start.9 = (bf16[1,128,1024]{2,1,0:T(8,128)(2,1)S(1)}, bf16[1,128,1024]{2,1,0:T(8,128)(2,1)}, u32[]{:S(2)}, u32[]{:S(2)}) collective-permute-start(bf16[1,128,1024]{2,1,0:T(8,128)(2,1)S(1)} %bitcast.100), channel_id=1, source_target_pairs={{16,0},{32,16},{48,32},{64,48},{80,64},{96,80},{112,96},{128,112},... | collective-permute-start | bytes 786440 | tf_op jit(solution)/shard_map/ppermute | solution.py:22
  115.5 1.9 %collective-permute-start.8 = (bf16[1,128,1024]{2,1,0:T(8,128)(2,1)S(1)}, bf16[1,128,1024]{2,1,0:T(8,128)(2,1)}, u32[]{:S(2)}, u32[]{:S(2)}) collective-permute-start(bf16[1,128,1024]{2,1,0:T(8,128)(2,1)S(1)} %bitcast.101), channel_id=1, source_target_pairs={{0,16},{16,32},{32,48},{48,64},{64,80},{80,96},{96,112},{112,128},... | collective-permute-start | bytes 786440 | tf_op jit(solution)/shard_map/ppermute | solution.py:20
  117.4 0.8 copy.104
  118.2 1.1 copy.78
  119.3 1.5 %fusion.9 = f32[8,128]{1,0:T(8,128)S(1)} fusion(bf16[384,8,128]{0,2,1:T(8,128)(2,1)} %bitcast.98, f32[8,384,128]{2,1,0:T(8,128)S(1)} %get-tuple-element.16, f32[8,128]{1,0:T(8,128)S(1)} %log_add_fusion, bf16[128,8,128]{0,2,1:T(8,128)(2,1)S(1)} %copy.78), kind=kOutput, calls=%fused_computation.20 | convolution fusion | flops 101841920 | bytes 2629632 | tf_op jit(solution)/shard_map/hqk,khd->hqd/dot_general | solution.py:83
  120.9 5.8 %collective-permute-start.11 = (f32[1,128,8]{1,2,0:T(8,128)S(1)}, f32[1,128,8]{1,2,0:T(8,128)S(1)}, u32[]{:S(2)}, u32[]{:S(2)}) collective-permute-start(f32[1,128,8]{1,2,0:T(8,128)S(1)} %bitcast.120), channel_id=1, source_target_pairs={{16,0},{32,16},{48,32},{64,48},{80,64},{96,80},{112,96},{128,112},... | collective-permute-start | bytes 12296 | tf_op jit(solution)/shard_map/ppermute | solution.py:22
  126.6 1.9 %collective-permute-start.10 = (f32[1,128,8]{1,2,0:T(8,128)S(1)}, f32[1,128,8]{1,2,0:T(8,128)S(1)}, u32[]{:S(2)}, u32[]{:S(2)}) collective-permute-start(f32[1,128,8]{1,2,0:T(8,128)S(1)} %bitcast.121), channel_id=1, source_target_pairs={{0,16},{16,32},{32,48},{48,64},{64,80},{80,96},{96,112},{112,128},... | collective-permute-start | bytes 12296 | tf_op jit(solution)/shard_map/ppermute | solution.py:20
  128.6 1.9 %fusion.7 = bf16[8,128,128]{2,1,0:T(8,128)(2,1)S(1)} fusion(bf16[384,8,128]{0,2,1:T(8,128)(2,1)S(1)} %bitcast.97, bf16[384,8,128]{0,2,1:T(8,128)(2,1)} %bitcast.99, f32[8,384,128]{2,1,0:T(8,128)S(1)} %get-tuple-element.16, f32[8,128]{1,0:T(8,128)S(1)} %fusion.9, f32[8,128]{1,0:T(8,128)S(1)} %log_add_fusion, bf16[128,1024]{1,0:T(8,128)(2,1)S(1)} %convolution_convert_fusion.1), kind=kOutput, calls=%fused_computation.16 | convolution fusion | flops 203161600 | bytes 3678208 | tf_op jit(solution)/shard_map/hqk,khd->qhd/dot_general | solution.py:88
  130.5 0.9 copy.92
  131.3 2.4 %collective-permute-done.10 = f32[1,128,8]{1,2,0:T(8,128)S(1)} collective-permute-done((f32[1,128,8]{1,2,0:T(8,128)S(1)}, f32[1,128,8]{1,2,0:T(8,128)S(1)}, u32[]{:S(2)}, u32[]{:S(2)}) %collective-permute-start.10) | collective-permute-done | bytes 4128 | tf_op jit(solution)/shard_map/ppermute | solution.py:20
  133.7 1.0 copy.107
  134.7 1.0 copy.106
  135.7 0.8 copy_dynamic-update-slice_fusion.1
  136.5 0.8 bitcast_dynamic-update-slice_fusion
  137.2 0.8 copy_dynamic-update-slice_fusion
  138.0 2.1 %convolution_convert_fusion = bf16[8,128,128]{2,1,0:T(8,128)(2,1)S(1)} fusion(bf16[384,8,128]{2,0,1:T(8,128)(2,1)} %copy_dynamic-update-slice_fusion, f32[8,384,128]{2,1,0:T(8,128)S(1)} %copy-done.3, f32[8,384]{1,0:T(8,128)S(1)} %maximum_bitcast_fusion, pred[384,128]{1,0:T(8,128)(4,1)S(1)} %broadcast_and_fusion), kind=kOutput, calls=%fused_computation.17 | convolution fusion | flops 102367232 | bytes 2682880 | tf_op jit(solution)/shard_map/hqk,qhd->khd/dot_general | solution.py:119
  140.2 0.9 copy.94
  141.0 2.2 %fusion.6 = bf16[8,128,128]{2,1,0:T(8,128)(2,1)S(1)} fusion(bf16[384,8,128]{0,2,1:T(8,128)(2,1)S(1)} %bitcast.104, f32[8,384,128]{2,1,0:T(8,128)S(1)} %copy-done.3, f32[8,384]{1,0:T(8,128)S(1)} %maximum_bitcast_fusion.1, f32[8,384]{1,0:T(8,128)S(1)} %maximum_bitcast_fusion, pred[384,128]{1,0:T(8,128)(4,1)S(1)} %broadcast_and_fusion, ...), kind=kOutput, calls=%fused_computation.15 | convolution fusion | flops 203948032 | bytes 3743744 | tf_op jit(solution)/shard_map/hqk,qhd->khd/dot_general | solution.py:117
  143.3 0.9 copy.93
  (41 shorter events, 0.3 us)
Async XLA Ops:
  7.2 97.3 %copy-start = (bf16[1,128,2048]{2,1,0:T(8,128)(2,1)S(1)}, bf16[1,128,2048]{2,1,0:T(8,128)(2,1)}, u32[]{:S(2)}) copy-start(bf16[1,128,2048]{2,1,0:T(8,128)(2,1)} %param.10) | copy-start | bytes 1572868
  7.2 35.1 %copy-start.4 = (bf16[1,128,1024]{2,1,0:T(8,128)(2,1)S(1)}, bf16[1,128,1024]{2,1,0:T(8,128)(2,1)}, u32[]{:S(2)}) copy-start(bf16[1,128,1024]{2,1,0:T(8,128)(2,1)} %param.9) | copy-start | bytes 786436
  7.2 35.9 %copy-start.5 = (bf16[1,128,1024]{2,1,0:T(8,128)(2,1)S(1)}, bf16[1,128,1024]{2,1,0:T(8,128)(2,1)}, u32[]{:S(2)}) copy-start(bf16[1,128,1024]{2,1,0:T(8,128)(2,1)} %param.8) | copy-start | bytes 786436
  7.2 35.9 %copy-start.6 = (bf16[1,128,1024]{2,1,0:T(8,128)(2,1)S(1)}, bf16[1,128,1024]{2,1,0:T(8,128)(2,1)}, u32[]{:S(2)}) copy-start(bf16[1,128,1024]{2,1,0:T(8,128)(2,1)} %param.7) | copy-start | bytes 786436
  7.2 34.3 %copy-start.8 = (s32[48,4]{0,1:T(4,128)S(1)}, s32[48,4]{0,1:T(4,128)}, u32[]{:S(2)}) copy-start(s32[48,4]{0,1:T(4,128)} %param.12) | copy-start | bytes 2308
  7.2 34.7 %copy-start.9 = (s32[1,48]{1,0:T(1,128)S(1)}, s32[1,48]{1,0:T(1,128)}, u32[]{:S(2)}) copy-start(s32[1,48]{1,0:T(1,128)} %param.13) | copy-start | bytes 580
  7.2 97.2 %all-gather.2.cloned.1.call-start = ((), (), s32[]{:S(2)}) async-start(), calls=%async_computation | async-start | bytes 4456448 | tf_op jit(solution)/shard_map/all_gather | solution.py:65
  9.1 47.4 %collective-permute-start.3 = (bf16[1,128,1024]{1,2,0:T(8,128)(2,1)S(1)}, bf16[1,128,1024]{1,2,0:T(8,128)(2,1)}, u32[]{:S(2)}, u32[]{:S(2)}) collective-permute-start(bf16[1,128,1024]{1,2,0:T(8,128)(2,1)S(1)} %copy.73), channel_id=1, source_target_pairs={{16,0},{32,16},{48,32},{64,48},{80,64},{96,80},{112,96},{128,112},... | collective-permute-start | bytes 786440 | tf_op jit(solution)/shard_map/ppermute | solution.py:22
  23.9 32.6 %collective-permute-start.2 = (bf16[1,128,1024]{1,2,0:T(8,128)(2,1)S(1)}, bf16[1,128,1024]{1,2,0:T(8,128)(2,1)}, u32[]{:S(2)}, u32[]{:S(2)}) collective-permute-start(bf16[1,128,1024]{1,2,0:T(8,128)(2,1)S(1)} %copy.73), channel_id=1, source_target_pairs={{0,16},{16,32},{32,48},{48,64},{64,80},{80,96},{96,112},{112,128},... | collective-permute-start | bytes 786440 | tf_op jit(solution)/shard_map/ppermute | solution.py:20
  27.0 16.3 %collective-permute-start.1 = (bf16[1,128,1024]{1,2,0:T(8,128)(2,1)S(1)}, bf16[1,128,1024]{1,2,0:T(8,128)(2,1)S(1)}, u32[]{:S(2)}, u32[]{:S(2)}) collective-permute-start(bf16[1,128,1024]{1,2,0:T(8,128)(2,1)S(1)} %copy.68), channel_id=1, source_target_pairs={{16,0},{32,16},{48,32},{64,48},{80,64},{96,80},{112,96},{128,112},... | collective-permute-start | bytes 786440 | tf_op jit(solution)/shard_map/ppermute | solution.py:22
  32.7 12.5 %collective-permute-start = (bf16[1,128,1024]{1,2,0:T(8,128)(2,1)S(1)}, bf16[1,128,1024]{1,2,0:T(8,128)(2,1)S(1)}, u32[]{:S(2)}, u32[]{:S(2)}) collective-permute-start(bf16[1,128,1024]{1,2,0:T(8,128)(2,1)S(1)} %copy.68), channel_id=1, source_target_pairs={{0,16},{16,32},{32,48},{48,64},{64,80},{80,96},{96,112},{112,128},... | collective-permute-start | bytes 786440 | tf_op jit(solution)/shard_map/ppermute | solution.py:20
  35.8 16.1 %collective-permute-start.5 = (bf16[1,128,1024]{1,2,0:T(8,128)(2,1)S(1)}, bf16[1,128,1024]{1,2,0:T(8,128)(2,1)}, u32[]{:S(2)}, u32[]{:S(2)}) collective-permute-start(bf16[1,128,1024]{1,2,0:T(8,128)(2,1)S(1)} %copy.82), channel_id=1, source_target_pairs={{16,0},{32,16},{48,32},{64,48},{80,64},{96,80},{112,96},{128,112},... | collective-permute-start | bytes 786440 | tf_op jit(solution)/shard_map/ppermute | solution.py:22
  43.3 10.5 %collective-permute-start.4 = (bf16[1,128,1024]{1,2,0:T(8,128)(2,1)S(1)}, bf16[1,128,1024]{1,2,0:T(8,128)(2,1)S(1)}, u32[]{:S(2)}, u32[]{:S(2)}) collective-permute-start(bf16[1,128,1024]{1,2,0:T(8,128)(2,1)S(1)} %copy.82), channel_id=1, source_target_pairs={{0,16},{16,32},{32,48},{48,64},{64,80},{80,96},{96,112},{112,128},... | collective-permute-start | bytes 786440 | tf_op jit(solution)/shard_map/ppermute | solution.py:20
  46.1 12.5 %collective-permute-start.7 = (f32[1,128,8]{1,2,0:T(8,128)S(1)}, f32[1,128,8]{1,2,0:T(8,128)S(1)}, u32[]{:S(2)}, u32[]{:S(2)}) collective-permute-start(f32[1,128,8]{1,2,0:T(8,128)S(1)} %bitcast.117), channel_id=1, source_target_pairs={{16,0},{32,16},{48,32},{64,48},{80,64},{96,80},{112,96},{128,112},... | collective-permute-start | bytes 12296 | tf_op jit(solution)/shard_map/ppermute | solution.py:22
  51.9 7.0 %collective-permute-start.6 = (f32[1,128,8]{1,2,0:T(8,128)S(1)}, f32[1,128,8]{1,2,0:T(8,128)S(1)}, u32[]{:S(2)}, u32[]{:S(2)}) collective-permute-start(f32[1,128,8]{1,2,0:T(8,128)S(1)} %bitcast.118), channel_id=1, source_target_pairs={{0,16},{16,32},{32,48},{48,64},{64,80},{80,96},{96,112},{112,128},... | collective-permute-start | bytes 12296 | tf_op jit(solution)/shard_map/ppermute | solution.py:20
  54.9 3.7 %copy-start.1 = (bf16[1,384,1024]{1,2,0:T(8,128)(2,1)}, bf16[1,384,1024]{1,2,0:T(8,128)(2,1)S(1)}, u32[]{:S(2)}) copy-start(bf16[1,384,1024]{1,2,0:T(8,128)(2,1)S(1)} %pad_maximum_fusion.2) | copy-start | bytes 2359300
  108.1 25.6 %collective-permute-start.9 = (bf16[1,128,1024]{2,1,0:T(8,128)(2,1)S(1)}, bf16[1,128,1024]{2,1,0:T(8,128)(2,1)}, u32[]{:S(2)}, u32[]{:S(2)}) collective-permute-start(bf16[1,128,1024]{2,1,0:T(8,128)(2,1)S(1)} %bitcast.100), channel_id=1, source_target_pairs={{16,0},{32,16},{48,32},{64,48},{80,64},{96,80},{112,96},{128,112},... | collective-permute-start | bytes 786440 | tf_op jit(solution)/shard_map/ppermute | solution.py:22
  115.5 19.2 %collective-permute-start.8 = (bf16[1,128,1024]{2,1,0:T(8,128)(2,1)S(1)}, bf16[1,128,1024]{2,1,0:T(8,128)(2,1)}, u32[]{:S(2)}, u32[]{:S(2)}) collective-permute-start(bf16[1,128,1024]{2,1,0:T(8,128)(2,1)S(1)} %bitcast.101), channel_id=1, source_target_pairs={{0,16},{16,32},{32,48},{48,64},{64,80},{80,96},{96,112},{112,128},... | collective-permute-start | bytes 786440 | tf_op jit(solution)/shard_map/ppermute | solution.py:20
  120.9 10.4 %collective-permute-start.11 = (f32[1,128,8]{1,2,0:T(8,128)S(1)}, f32[1,128,8]{1,2,0:T(8,128)S(1)}, u32[]{:S(2)}, u32[]{:S(2)}) collective-permute-start(f32[1,128,8]{1,2,0:T(8,128)S(1)} %bitcast.120), channel_id=1, source_target_pairs={{16,0},{32,16},{48,32},{64,48},{80,64},{96,80},{112,96},{128,112},... | collective-permute-start | bytes 12296 | tf_op jit(solution)/shard_map/ppermute | solution.py:22
  126.6 7.0 %collective-permute-start.10 = (f32[1,128,8]{1,2,0:T(8,128)S(1)}, f32[1,128,8]{1,2,0:T(8,128)S(1)}, u32[]{:S(2)}, u32[]{:S(2)}) collective-permute-start(f32[1,128,8]{1,2,0:T(8,128)S(1)} %bitcast.121), channel_id=1, source_target_pairs={{0,16},{16,32},{32,48},{48,64},{64,80},{80,96},{96,112},{112,128},... | collective-permute-start | bytes 12296 | tf_op jit(solution)/shard_map/ppermute | solution.py:20
  130.5 7.6 %copy-start.3 = (f32[8,384,128]{2,1,0:T(8,128)S(1)}, f32[8,384,128]{2,1,0:T(8,128)}, u32[]{:S(2)}) copy-start(f32[8,384,128]{2,1,0:T(8,128)} %fusion.33) | copy-start | bytes 4718596
  138.0 3.0 %copy-start.2 = (bf16[1,384,1024]{1,2,0:T(8,128)(2,1)S(1)}, bf16[1,384,1024]{1,2,0:T(8,128)(2,1)}, u32[]{:S(2)}) copy-start(bf16[1,384,1024]{1,2,0:T(8,128)(2,1)} %copy-done.1) | copy-start | bytes 2359300
  138.0 3.0 %copy-start.7 = (bf16[16,8,8,128]{3,2,1,0:T(8,128)(2,1)S(1)}, bf16[16,8,8,128]{3,2,1,0:T(8,128)(2,1)}, u32[]{:S(2)}) copy-start(bf16[16,8,8,128]{3,2,1,0:T(8,128)(2,1)} %copy.108) | copy-start | bytes 786436
Sparse Core Ops, SparseCore 0:
  11.7 92.7 all-gather.1
where the time goes:
time: 152 us; the launch traced here: 151 us
  starting transfers between devices  56.7 us (37%)
  waiting for transfers between devices  48.9 us (32%)
  between operations  14.4 us (9%)
  matrix products  13.6 us (9%)
  local copies, waits for them, and re-layouts  13.3 us (9%)
  other arithmetic  4.03 us (3%)
    all_gather x1, waiting for transfers between devices, body(): lax.all_gather(w_out, 'fsdp', axis=0, tiled=True)  45.5 us
    ppermute x6, starting transfers between devices, with_halo(): lax.ppermute(head, axis, [((i + 1) % count, i) for i in range(ends)])  45.2 us
    ppermute x6, starting transfers between devices, with_halo(): lax.ppermute(tail, axis, [(i, (i + 1) % count) for i in range(ends)])  11.5 us
    unnamed x34, local copies, waits for them, and re-layouts  11.1 us
    dot_general x1, matrix products, body(): jnp.einsum('td,rd->tr', cotangent_rows, lax.all_gather(w_out, 'fsdp', axi...  3.7 us
    concatenate x3, other arithmetic, with_halo(): jnp.concatenate([lax.ppermute(tail, axis, [(i, (i + 1) % count) for i in...  3.21 us
  transfers between devices with their start and end apart: 13, of which 3 were waited for; matrix products, arithmetic and copies ran while one was open for 12% of the time, Pallas kernels for 0%

commit v1 on v0

v1 whole, which is shorter than its diff:
```python
import functools

import jax
import jax.numpy as jnp
from jax import lax
from jax.experimental import pallas as pl
from jax.experimental.pallas import tpu as pltpu
from jax.sharding import PartitionSpec as P

HEADS = 8
HD = 128
TOK = 128
N_SEQ = 48
HALF_SEQ = 24
D = 2048
SCALE = HD ** (-0.5)
MESH = pl.DeviceIdType.MESH
ORDER = (0, 1, 3, 2)
BF = jnp.bfloat16
F32 = jnp.float32


def nt(a, b):
    return lax.dot_general(a, b, (((1,), (1,)), ((), ())), preferred_element_type=F32)


def tn(a, b):
    return lax.dot_general(a, b, (((0,), (0,)), ((), ())), preferred_element_type=F32)


def nn(a, b):
    return lax.dot_general(a, b, (((1,), (0,)), ((), ())), preferred_element_type=F32)


def kernel(
    pat_ref, val_ref, q_hbm, k_hbm, v_hbm, do_hbm, w_ref,
    dq_ref, dk_ref, dv_ref,
    q_ref, k_ref, v_ref, do_ref, wf, kh, vh, qh, dh, sth, d_own, st_own, prob, dk_acc, dv_acc,
    wr, sx, sy, ssib, hs_s, hs_r, ds_s, ds_r, ts_s, ts_r, lsem, isem,
):
    p = lax.axis_index("seq")
    f = lax.axis_index("fsdp")
    core = p % 2
    low = p // HALF_SEQ
    k_y = f // 4
    x = f % 4
    sgn = 2 * low - 1
    sib = (p + 1 - 2 * core, f)
    other_y = p + HALF_SEQ * (1 - 2 * low)
    xr = (p, k_y * 4 + (x + 1) % 4)
    xl = (p, k_y * 4 + (x + 3) % 4)
    inter = (other_y, ((k_y + sgn + 4) % 4) * 4 + x)
    intra = (other_y, f)
    opp = (other_y, ((k_y + 2) % 4) * 4 + x)
    has_l = p > 0
    has_r = p < N_SEQ - 1
    left = (p - 1, f)
    right = (p + 1, f)

    loads = [
        pltpu.make_async_copy(a, b, isem.at[i])
        for i, (a, b) in enumerate(
            ((k_hbm, k_ref), (q_hbm, q_ref), (v_hbm, v_ref), (do_hbm, do_ref))
        )
    ]
    own_w = pltpu.make_async_copy(w_ref, wf.at[f], lsem)
    for copy in loads:
        copy.start()
    own_w.start()

    barrier = pltpu.get_barrier_semaphore()
    for dev in (sib, xr, xl, inter, intra, opp):
        pl.semaphore_signal(barrier, inc=1, device_id=dev, device_id_type=MESH)

    @pl.when((core == 0) & has_l)
    def _():
        pl.semaphore_signal(barrier, inc=1, device_id=left, device_id_type=MESH)

    @pl.when((core == 1) & has_r)
    def _():
        pl.semaphore_signal(barrier, inc=1, device_id=right, device_id_type=MESH)

    pl.semaphore_wait(barrier, 5 + (p + N_SEQ - 1) // N_SEQ + (2 * N_SEQ - 2 - p) // N_SEQ)

    def rcopy(src, dst, ssem, rsem, dev):
        return pltpu.make_async_remote_copy(
            src_ref=src, dst_ref=dst, send_sem=ssem, recv_sem=rsem,
            device_id=dev, device_id_type=MESH,
        )

    pending = []

    def put_own(ch, ssem, dev):
        c = rcopy(w_ref.at[ch], wf.at[f, ch], ssem, wr.at[f, ch], dev)
        c.start()
        pending.append(c)

    def put(sh, ch, ssem, dev):
        c = rcopy(wf.at[sh, ch], wf.at[sh, ch], ssem, wr.at[sh, ch], dev)
        c.start()
        pending.append(c)

    def wait_w(sh, ch):
        rcopy(wf.at[sh, ch], wf.at[sh, ch], lsem, wr.at[sh, ch], sib).wait_recv()

    def shard(s, dx):
        return ((k_y + sgn * ORDER[s] + 4) % 4) * 4 + (x + dx) % 4

    mine = (2 * core, 2 * core + 1)
    theirs = (2 - 2 * core, 3 - 2 * core)

    for i in range(2):
        put_own(mine[i], sy.at[i], inter)
        put_own(mine[i], sx.at[0, 0, i], xr)
        put_own(mine[i], sx.at[1, 0, i], xl)
    for i in range(2):
        put_own(mine[i], sy.at[2 + i], opp)

    def halo(i, src, dst, side, dev):
        return rcopy(src.at[0], dst.at[1 - side], hs_s.at[side, i], hs_r.at[1 - side, i], dev)

    halo_parts = ((0, k_hbm, kh), (1, q_hbm, qh), (2, v_hbm, vh))

    @pl.when(has_l)
    def _():
        for i, src, dst in halo_parts:
            halo(i, src, dst, 0, left).start()

    @pl.when(has_r)
    def _():
        for i, src, dst in halo_parts:
            halo(i, src, dst, 1, right).start()

    def clear(side):
        for buf in (kh, vh, qh):
            buf[side] = jnp.zeros((TOK, HEADS * HD), BF)
        dh[side] = jnp.zeros((HEADS, TOK, HD), BF)
        sth[side] = jnp.zeros((HEADS, 8, 128), F32)

    @pl.when(p == 0)
    def _():
        clear(0)

    @pl.when(p == N_SEQ - 1)
    def _():
        clear(1)

    def limit(qb, kb, ok):
        row = (qb + N_SEQ) % N_SEQ
        hit = pat_ref[0, row] == kb
        for i in range(1, 4):
            hit = hit | (pat_ref[i, row] == kb)
        return jnp.where(hit & ok, val_ref[0, (kb + N_SEQ) % N_SEQ], 0)

    lim_own = (limit(p, p - 1, has_l), limit(p, p, p >= 0), limit(p, p + 1, has_r))
    lim_far = (limit(p - 1, p, has_l), limit(p + 1, p, has_r))

    def masked(score, lim):
        rows = lax.broadcasted_iota(jnp.int32, (TOK, TOK), 0)
        return jnp.where(rows < lim, score * SCALE, -jnp.inf)

    def head_of(t):
        s = t // 2
        turn = s + (s // 2) * (1 - 2 * (s % 2))
        return ((k_y + sgn * turn + 4) % 4) * 2 + (x // 2 + t) % 2

    def lanes(h):
        return pl.ds(pl.multiple_of(h * HD, HD), HD)

    def early(t, carry):
        h = head_of(t)
        c = lanes(h)
        q = q_ref[0, :, c]
        s0 = masked(nt(kh[0, :, c], q), lim_own[0])
        s1 = masked(nt(k_ref[0, :, c], q), lim_own[1])
        s2 = masked(nt(kh[1, :, c], q), lim_own[2])
        top = jnp.max(jnp.maximum(jnp.maximum(s0, s1), s2), axis=0, keepdims=True)
        e0, e1, e2 = jnp.exp(s0 - top), jnp.exp(s1 - top), jnp.exp(s2 - top)
        total = jnp.sum(e0 + e1 + e2, axis=0, keepdims=True)
        inv = 1.0 / total
        prob[h, 0] = e0 * inv
        prob[h, 1] = e1 * inv
        prob[h, 2] = e2 * inv
        st_own[h, 0:1, :] = top + jnp.log(total)
        return carry

    def sends(h, fn):
        @pl.when(has_l)
        def _():
            fn(rcopy(d_own.at[h], dh.at[1, h], ds_s.at[0, h], ds_r.at[1, h], left))
            fn(rcopy(st_own.at[h], sth.at[1, h], ts_s.at[0, h], ts_r.at[1, h], left))

        @pl.when(has_r)
        def _():
            fn(rcopy(d_own.at[h], dh.at[0, h], ds_s.at[1, h], ds_r.at[0, h], right))
            fn(rcopy(st_own.at[h], sth.at[0, h], ts_s.at[1, h], ts_r.at[0, h], right))

    def own_head(t, carry):
        h = head_of(t)
        c = lanes(h)
        w_h = wf[pl.ds(2 * h, 2)].reshape(HD, D)
        d = nt(do_ref[0], w_h).astype(BF)
        d_own[h] = d
        dp = (nt(vh[0, :, c], d), nt(v_ref[0, :, c], d), nt(vh[1, :, c], d))
        pr = (prob[h, 0], prob[h, 1], prob[h, 2])
        prb = tuple(a.astype(BF) for a in pr)
        delta = jnp.sum(
            prb[0].astype(F32) * dp[0] + prb[1].astype(F32) * dp[1] + prb[2].astype(F32) * dp[2],
            axis=0, keepdims=True,
        )
        st_own[h, 1:2, :] = delta
        sends(h, lambda copy: copy.start())
        ds = tuple((a * (b - delta)).astype(BF) for a, b in zip(pr, dp))
        k_own = k_ref[0, :, c]
        dq = tn(ds[0], kh[0, :, c]) + tn(ds[1], k_own) + tn(ds[2], kh[1, :, c])
        dq_ref[0, :, c] = (dq * SCALE).astype(BF)
        dk_acc[h] = nn(ds[1], q_ref[0, :, c])
        dv_acc[h] = nn(prb[1], d)
        return carry

    def far_head(t, carry):
        h = head_of(t)
        c = lanes(h)

        @pl.when(has_l)
        def _():
            rcopy(d_own.at[h], dh.at[0, h], ds_s.at[1, h], ds_r.at[0, h], sib).wait_recv()
            rcopy(st_own.at[h], sth.at[0, h], ts_s.at[1, h], ts_r.at[0, h], sib).wait_recv()

        @pl.when(has_r)
        def _():
            rcopy(d_own.at[h], dh.at[1, h], ds_s.at[0, h], ds_r.at[1, h], sib).wait_recv()
            rcopy(st_own.at[h], sth.at[1, h], ts_s.at[0, h], ts_r.at[1, h], sib).wait_recv()

        k_own = k_ref[0, :, c]
        v_own = v_ref[0, :, c]
        dk = dk_acc[h]
        dv = dv_acc[h]
        for side in range(2):
            q = qh[side, :, c]
            d = dh[side, h]
            pr = jnp.exp(masked(nt(k_own, q), lim_far[side]) - sth[side, h, 0:1, :])
            ds = (pr * (nt(v_own, d) - sth[side, h, 1:2, :])).astype(BF)
            dk = dk + nn(ds, q)
            dv = dv + nn(pr.astype(BF), d)
        dk_ref[0, :, c] = (dk * SCALE).astype(BF)
        dv_ref[0, :, c] = dv.astype(BF)
        return carry

    def wait_halo():
        @pl.when(has_l)
        def _():
            for i, src, dst in halo_parts:
                rcopy(src.at[0], dst.at[0], hs_s.at[1, i], hs_r.at[0, i], sib).wait_recv()

        @pl.when(has_r)
        def _():
            for i, src, dst in halo_parts:
                rcopy(src.at[0], dst.at[1], hs_s.at[0, i], hs_r.at[1, i], sib).wait_recv()

    def y_round(s):
        for i in range(2):
            sh, ch = shard(s, 0), mine[i]
            wait_w(sh, ch)
            if s == 1:
                put(sh, ch, sy.at[4 + i], intra)
            put(sh, ch, sx.at[0, s, i], xr)
            put(sh, ch, sx.at[1, s, i], xl)
            put(sh, ch, ssib.at[s, i], sib)

    def x_round(s):
        for i in range(2):
            for side, dx in ((0, 3), (1, 1)):
                sh, ch = shard(s, dx), mine[i]
                wait_w(sh, ch)
                if i == side:
                    put(sh, ch, sx.at[side, s, 2], xr if side == 0 else xl)
                put(sh, ch, ssib.at[s, 2 + 2 * side + i], sib)

    def far_round(s):
        for i in range(2):
            sh, ch = shard(s, 2), mine[i]
            wait_w(sh, ch)
            put(sh, ch, ssib.at[s, 6 + i], sib)

    def sib_round(s, which):
        for dx in which:
            if s == 0 and dx == 0:
                continue
            for i in range(2):
                wait_w(shard(s, dx), theirs[i])

    y_round(1)
    x_round(0)
    y_round(2)
    for copy in loads:
        copy.wait()
    wait_halo()
    lax.fori_loop(0, 2, early, 0)
    x_round(1)
    y_round(3)
    far_round(0)
    own_w.wait()
    sib_round(0, (0, 1, 2, 3))
    lax.fori_loop(0, 2, own_head, 0)
    x_round(2)
    far_round(1)
    lax.fori_loop(2, 6, early, 0)
    sib_round(1, (0, 1, 2, 3))
    lax.fori_loop(2, 4, own_head, 0)
    lax.fori_loop(0, 2, far_head, 0)
    x_round(3)
    far_round(2)
    lax.fori_loop(6, 8, early, 0)
    sib_round(2, (0, 1, 2, 3))
    lax.fori_loop(4, 6, own_head, 0)
    far_round(3)
    lax.fori_loop(2, 6, far_head, 0)
    sib_round(3, (0, 1, 2, 3))
    lax.fori_loop(6, 8, own_head, 0)
    lax.fori_loop(6, 8, far_head, 0)

    for c in pending:
        c.wait_send()

    @pl.when(has_l)
    def _():
        for i, src, dst in halo_parts:
            halo(i, src, dst, 0, left).wait_send()

    @pl.when(has_r)
    def _():
        for i, src, dst in halo_parts:
            halo(i, src, dst, 1, right).wait_send()

    def drain(h, carry):
        sends(h, lambda copy: copy.wait_send())
        return carry

    lax.fori_loop(0, HEADS, drain, 0)


def body(queries, keys, values, d_out, w_out, pattern, valid):
    tok, width = queries.shape[1], queries.shape[2]
    vm = pl.BlockSpec(memory_space=pltpu.VMEM)
    sm = pl.BlockSpec(memory_space=pltpu.SMEM)
    hbm = pl.BlockSpec(memory_space=pltpu.HBM)
    out = jax.ShapeDtypeStruct((1, tok, width), BF)
    dma = pltpu.SemaphoreType.DMA
    return pl.pallas_call(
        kernel,
        out_shape=(out, out, out),
        in_specs=[sm, sm, hbm, hbm, hbm, hbm, hbm],
        out_specs=(vm, vm, vm),
        scratch_shapes=[
            pltpu.VMEM((1, tok, width), BF),
            pltpu.VMEM((1, tok, width), BF),
            pltpu.VMEM((1, tok, width), BF),
            pltpu.VMEM((1, tok, D), BF),
            pltpu.VMEM((16, 4, 16, D), BF),
            pltpu.VMEM((2, tok, width), BF),
            pltpu.VMEM((2, tok, width), BF),
            pltpu.VMEM((2, tok, width), BF),
            pltpu.VMEM((2, HEADS, tok, HD), BF),
            pltpu.VMEM((2, HEADS, 8, 128), F32),
            pltpu.VMEM((HEADS, tok, HD), BF),
            pltpu.VMEM((HEADS, 8, 128), F32),
            pltpu.VMEM((HEADS, 3, tok, tok), F32),
            pltpu.VMEM((HEADS, tok, HD), F32),
            pltpu.VMEM((HEADS, tok, HD), F32),
            dma((16, 4)),
            dma((2, 4, 3)),
            dma((6,)),
            dma((4, 8)),
            dma((2, 3)),
            dma((2, 3)),
            dma((2, HEADS)),
            dma((2, HEADS)),
            dma((2, HEADS)),
            dma((2, HEADS)),
            dma,
            dma((4,)),
        ],
        compiler_params=pltpu.CompilerParams(
            collective_id=0, has_side_effects=True
        ),
        name="attention_backward",
    )(pattern.T, valid, queries, keys, values, d_out, w_out.reshape(4, 16, D))


def solution(mesh):
    spec = P("fsdp", "seq", None)
    in_specs = (spec, spec, spec, spec, P("fsdp", None), P(), P("fsdp", None))
    return jax.shard_map(
        body, mesh=mesh, in_specs=in_specs, out_specs=(spec, spec, spec), check_vma=False
    )
```

time: 152 us -> 62.1 us (0.41)
  Pallas kernels: 0 us -> 57.3 us
  starting transfers between devices: 56.7 us -> 0 us
  waiting for transfers between devices: 48.9 us -> 0 us
  between operations: 14.4 us -> 0.65 us
  matrix products: 13.6 us -> 0 us
  local copies, waits for them, and re-layouts: 13.3 us -> 3.46 us
  other arithmetic: 4.03 us -> 0 us
    pallas_call x0 -> x1, Pallas kernels: none -> 57.3 us  [body(): pl.pallas_call(kernel, out_shape=(out, out, out), in_specs=[sm, sm, hbm,...]
    ppermute x12 -> x0, starting transfers between devices: 56.7 us -> none  [the longest x6 45.2 us: with_halo(): lax.ppermute(head, axis, [((i + 1) % count, i) for i in range(ends)])]
    all_gather x1 -> x0, waiting for transfers between devices: 45.5 us -> none  [body(): lax.all_gather(w_out, 'fsdp', axis=0, tiled=True)]
    dot_general x7 -> x0, matrix products: 13.6 us -> none  [the longest x1 3.7 us: body(): jnp.einsum('td,rd->tr', cotangent_rows, lax.all_gather(w_out, 'fsdp', axi...]
    unnamed x34 -> x7, local copies, waits for them, and re-layouts: 11.1 us -> 3.46 us
    concatenate x3 -> x0, other arithmetic: 3.21 us -> none  [with_halo(): jnp.concatenate([lax.ppermute(tail, axis, [(i, (i + 1) % count) for i in...]
    ppermute x12 -> x0, waiting for transfers between devices: 2.74 us -> none  [the longest x6 2.72 us: with_halo(): lax.ppermute(tail, axis, [(i, (i + 1) % count) for i in range(ends)])]
  transfers between devices with their start and end apart: 13 -> 0, of which waited for: 3 -> 0; matrix products, arithmetic and copies ran while one was open for 12% -> 0% of each run, Pallas kernels for 0% -> 0%
where the time goes in v1:
time: 62.1 us; the launch traced here: 61.4 us
  Pallas kernels  57.3 us (92%)
  local copies, waits for them, and re-layouts  3.46 us (6%)
  between operations  0.65 us (1%)
    pallas_call x1, Pallas kernels, body(): pl.pallas_call(kernel, out_shape=(out, out, out), in_specs=[sm, sm, hbm,...  57.3 us
    unnamed x7, local copies, waits for them, and re-layouts  3.46 us

profile of v1, /device:TPU:56, one launch (start us, length us, event | category | flops | bytes accessed | tf_op | source)
XLA Modules:
  0.0 61.4 jit_solution(3715008195776218841)
XLA Ops:
  0.6 57.3 %attention_backward.1 = (bf16[1,128,1024]{2,1,0:T(8,128)(2,1)}, bf16[1,128,1024]{2,1,0:T(8,128)(2,1)}, bf16[1,128,1024]{2,1,0:T(8,128)(2,1)}) custom-call(s32[4,48]{1,0:T(4,128)} %bitcast.3, s32[1,48]{1,0:T(1,128)} %val_ref.1, bf16[1,128,1024]{2,1,0:T(8,128)(2,1)} %q_hbm.1, bf16[1,128,1024]{2,1,0:T(8,128)(2,1)} %k_hbm.1, bf16[1,128,1024]{2,1,0:T(8,128)(2,1)} %v_hbm.1, ...), custom_call_target="tpu_custom_call" | custom-call | tf_op jit(solution)/shard_map/attention_backward/pallas_call | solution.py:350
  58.0 0.0 copy-start.1
  58.0 1.7 %copy.13 = bf16[1,128,1024]{2,1,0:T(8,128)(2,1)} copy(bf16[1,128,1024]{2,1,0:T(8,128)(2,1)} %get-tuple-element.6) | data formatting | bytes 524288
  59.7 0.0 copy-done.1
  59.7 0.0 copy-start
  59.7 0.7 %copy.14 = bf16[1,128,1024]{2,1,0:T(8,128)(2,1)} copy(bf16[1,128,1024]{2,1,0:T(8,128)(2,1)S(1)} %copy-done.1) | data formatting | bytes 524288
  60.4 0.3 copy-done
  60.7 0.7 %copy.15 = bf16[1,128,1024]{2,1,0:T(8,128)(2,1)} copy(bf16[1,128,1024]{2,1,0:T(8,128)(2,1)S(1)} %copy-done) | data formatting | bytes 524288
Async XLA Ops:
  58.0 1.7 %copy-start.1 = (bf16[1,128,1024]{2,1,0:T(8,128)(2,1)S(1)}, bf16[1,128,1024]{2,1,0:T(8,128)(2,1)}, u32[]{:S(2)}) copy-start(bf16[1,128,1024]{2,1,0:T(8,128)(2,1)} %get-tuple-element.7) | copy-start | bytes 786436
  59.7 1.0 %copy-start = (bf16[1,128,1024]{2,1,0:T(8,128)(2,1)S(1)}, bf16[1,128,1024]{2,1,0:T(8,128)(2,1)}, u32[]{:S(2)}) copy-start(bf16[1,128,1024]{2,1,0:T(8,128)(2,1)} %get-tuple-element.8) | copy-start | bytes 786436

commit v2 on v1

v2 whole, which is shorter than its diff:
```python
import functools

import jax
import jax.numpy as jnp
from jax import lax
from jax.experimental import pallas as pl
from jax.experimental.pallas import tpu as pltpu
from jax.sharding import PartitionSpec as P

HEADS = 8
HD = 128
TOK = 128
N_SEQ = 48
HALF_SEQ = 24
D = 2048
SCALE = HD ** (-0.5)
MESH = pl.DeviceIdType.MESH
ORDER = (0, 1, 3, 2)
BF = jnp.bfloat16
F32 = jnp.float32


def nt(a, b):
    return lax.dot_general(a, b, (((1,), (1,)), ((), ())), preferred_element_type=F32)


def tn(a, b):
    return lax.dot_general(a, b, (((0,), (0,)), ((), ())), preferred_element_type=F32)


def nn(a, b):
    return lax.dot_general(a, b, (((1,), (0,)), ((), ())), preferred_element_type=F32)


def kernel(
    pat_ref, val_ref, q_hbm, k_hbm, v_hbm, do_hbm, w_ref,
    dq_ref, dk_ref, dv_ref,
    qb, kb, vb, do_ref, wf, dh, sth, d_own, st_own, prob, dk_acc, dv_acc, rel,
    wr, sx, sy, ssib, hs_s, hs_r, ds_s, ds_r, ts_s, ts_r, lsem, isem, ready, rel_r,
):
    p = lax.axis_index("seq")
    f = lax.axis_index("fsdp")
    core = p % 2
    low = p // HALF_SEQ
    k_y = f // 4
    x = f % 4
    sgn = 2 * low - 1
    sib = (p + 1 - 2 * core, f)
    zdev = (p - 1 + 2 * core, f)
    other_y = p + HALF_SEQ * (1 - 2 * low)
    xr = (p, k_y * 4 + (x + 1) % 4)
    xl = (p, k_y * 4 + (x + 3) % 4)
    inter = (other_y, ((k_y + sgn + 4) % 4) * 4 + x)
    intra = (other_y, f)
    opp = (other_y, ((k_y + 2) % 4) * 4 + x)
    has_l = p > 0
    has_r = p < N_SEQ - 1
    has_z = has_l & has_r
    wrap_lo = p == HALF_SEQ - 1
    wrap_hi = p == HALF_SEQ
    relays = p == 0
    wrap_dev = (HALF_SEQ - 1, f)
    greets_last = has_z & (((core == 0) & (p != HALF_SEQ)) | wrap_lo)
    greets_first = has_z & (((core == 1) & (p != HALF_SEQ - 1)) | wrap_hi)

    loads = [
        pltpu.make_async_copy(a, b, isem.at[i])
        for i, (a, b) in enumerate(
            (
                (k_hbm.at[0], kb.at[1]),
                (q_hbm.at[0], qb.at[1]),
                (v_hbm.at[0], vb.at[1]),
                (do_hbm.at[0], do_ref),
            )
        )
    ]
    own_w = pltpu.make_async_copy(w_ref, wf.at[f], lsem)
    for copy in loads:
        copy.start()
    own_w.start()

    barrier = pltpu.get_barrier_semaphore()
    for dev in (sib, xr, xl, inter, intra, opp):
        pl.semaphore_signal(barrier, inc=1, device_id=dev, device_id_type=MESH)

    @pl.when(greets_first)
    def _():
        pl.semaphore_signal(barrier, inc=1, device_id=zdev, device_id_type=MESH)

    @pl.when(relays)
    def _():
        pl.semaphore_signal(barrier, inc=1, device_id=wrap_dev, device_id_type=MESH)

    @pl.when(greets_last & ~wrap_lo)
    def _():
        pl.semaphore_wait(barrier, 7)
        pl.semaphore_signal(ready, inc=1, device_id=zdev, device_id_type=MESH)

    @pl.when(wrap_lo)
    def _():
        pl.semaphore_wait(barrier, 8)
        for dev in (zdev, (0, f)):
            pl.semaphore_signal(ready, inc=1, device_id=dev, device_id_type=MESH)

    @pl.when(~greets_last)
    def _():
        pl.semaphore_wait(barrier, 6)

    def rcopy(src, dst, ssem, rsem, dev):
        return pltpu.make_async_remote_copy(
            src_ref=src, dst_ref=dst, send_sem=ssem, recv_sem=rsem,
            device_id=dev, device_id_type=MESH,
        )

    pending = []

    def put_own(ch, ssem, dev):
        c = rcopy(w_ref.at[ch], wf.at[f, ch], ssem, wr.at[f, ch], dev)
        c.start()
        pending.append(c)

    def put(sh, ch, ssem, dev):
        c = rcopy(wf.at[sh, ch], wf.at[sh, ch], ssem, wr.at[sh, ch], dev)
        c.start()
        pending.append(c)

    def wait_w(sh, ch):
        rcopy(wf.at[sh, ch], wf.at[sh, ch], lsem, wr.at[sh, ch], sib).wait_recv()

    def shard(s, dx):
        return ((k_y + sgn * ORDER[s] + 4) % 4) * 4 + (x + dx) % 4

    mine = (2 * core, 2 * core + 1)
    theirs = (2 - 2 * core, 3 - 2 * core)

    for i in range(2):
        put_own(mine[i], sy.at[i], inter)
        put_own(mine[i], sx.at[0, 0, i], xr)
        put_own(mine[i], sx.at[1, 0, i], xl)
    for i in range(2):
        put_own(mine[i], sy.at[2 + i], opp)

    halo_parts = ((0, k_hbm, kb), (1, v_hbm, vb), (2, q_hbm, qb))

    def halo(i, src, dst, side, dev):
        return rcopy(
            src.at[0], dst.at[2 - 2 * side], hs_s.at[side, i], hs_r.at[1 - side, i], dev
        )

    def halo_to(side, dev):
        for i, src, dst in halo_parts:
            halo(i, src, dst, side, dev).start()

    halo_to(1 - core, sib)

    @pl.when(greets_last)
    def _():
        halo_to(core, zdev)

    @pl.when(greets_first & (p != HALF_SEQ))
    def _():
        pl.semaphore_wait(ready, 1)
        halo_to(core, zdev)

    def to_relay(i):
        return rcopy(halo_parts[i][1].at[0], rel.at[i], hs_s.at[0, i], rel_r.at[i], intra)

    def relay(i):
        dst = halo_parts[i][2].at[2]
        return rcopy(rel.at[i], dst, hs_s.at[0, i], hs_r.at[1, i], wrap_dev)

    def pass_on(i):
        @pl.when(relays)
        def _():
            if i == 0:
                pl.semaphore_wait(ready, 1)
            to_relay(i).wait_recv()
            relay(i).start()

    def wait_halo(which):
        for i in which:
            halo(*halo_parts[i], core, sib).wait_recv()

        @pl.when(has_z)
        def _():
            for i in which:
                halo(*halo_parts[i], 1 - core, sib).wait_recv()

    @pl.when(~has_z)
    def _():
        for buf in (kb, vb, qb):
            buf[2 * core] = jnp.zeros((TOK, HEADS * HD), BF)
        dh[core] = jnp.zeros((HEADS, TOK, HD), BF)
        sth[core] = jnp.zeros((HEADS, 8, 128), F32)

    def limit(qblock, kblock, ok):
        row = (qblock + N_SEQ) % N_SEQ
        hit = pat_ref[0, row] == kblock
        for i in range(1, 4):
            hit = hit | (pat_ref[i, row] == kblock)
        return jnp.where(hit & ok, val_ref[0, (kblock + N_SEQ) % N_SEQ], 0)

    lim_own = (limit(p, p - 1, has_l), limit(p, p, p >= 0), limit(p, p + 1, has_r))
    lim_far = (limit(p - 1, p, has_l), limit(p + 1, p, has_r))

    def masked(score, lim):
        rows = lax.broadcasted_iota(jnp.int32, (TOK, TOK), 0)
        return jnp.where(rows < lim, score * SCALE, -jnp.inf)

    def head_of(t):
        s = t // 2
        turn = s + (s // 2) * (1 - 2 * (s % 2))
        return ((k_y + sgn * turn + 4) % 4) * 2 + (x // 2 + t) % 2

    def lanes(h):
        return pl.ds(pl.multiple_of(h * HD, HD), HD)

    def thirds(a):
        return a[:TOK], a[TOK : 2 * TOK], a[2 * TOK :]

    def early(t, carry):
        h = head_of(t)
        c = lanes(h)
        score = nt(kb[:, :, c].reshape(3 * TOK, HD), qb[1, :, c])
        s0, s1, s2 = (masked(a, lim) for a, lim in zip(thirds(score), lim_own))
        top = jnp.max(jnp.maximum(jnp.maximum(s0, s1), s2), axis=0, keepdims=True)
        e0, e1, e2 = jnp.exp(s0 - top), jnp.exp(s1 - top), jnp.exp(s2 - top)
        total = jnp.sum(e0 + e1 + e2, axis=0, keepdims=True)
        inv = 1.0 / total
        prob[h, 0:TOK] = e0 * inv
        prob[h, TOK : 2 * TOK] = e1 * inv
        prob[h, 2 * TOK :] = e2 * inv
        st_own[h, 0:1, :] = top + jnp.log(total)
        return carry

    def send_d(h, side, dev):
        return (
            rcopy(d_own.at[h], dh.at[1 - side, h], ds_s.at[side, h], ds_r.at[1 - side, h], dev),
            rcopy(st_own.at[h], sth.at[1 - side, h], ts_s.at[side, h], ts_r.at[1 - side, h], dev),
        )

    def own_head(t, carry):
        h = head_of(t)
        c = lanes(h)
        w_h = wf[pl.ds(2 * h, 2)].reshape(HD, D)
        d = nt(do_ref[...], w_h).astype(BF)
        d_own[h] = d
        dp = nt(vb[:, :, c].reshape(3 * TOK, HD), d)
        pr = prob[h]
        prb = pr.astype(BF)
        delta = jnp.sum(prb.astype(F32) * dp, axis=0, keepdims=True)
        st_own[h, 1:2, :] = delta

        @pl.when(has_z)
        def _():
            for copy in send_d(h, core, zdev):
                copy.start()

        for copy in send_d(h, 1 - core, sib):
            copy.start()
        ds = (pr * (dp - delta)).astype(BF)
        dq = tn(ds, kb[:, :, c].reshape(3 * TOK, HD))
        dq_ref[0, :, c] = (dq * SCALE).astype(BF)
        dk_acc[h] = nn(ds[TOK : 2 * TOK], qb[1, :, c])
        dv_acc[h] = nn(prb[TOK : 2 * TOK], d)
        return carry

    def far_head(t, carry):
        h = head_of(t)
        c = lanes(h)
        for copy in send_d(h, core, sib):
            copy.wait_recv()

        @pl.when(has_z)
        def _():
            for copy in send_d(h, 1 - core, sib):
                copy.wait_recv()

        q = jnp.concatenate([qb[0, :, c], qb[2, :, c]], axis=0)
        d = dh[:, h].reshape(2 * TOK, HD)
        score = nt(kb[1, :, c], q)
        dp = nt(vb[1, :, c], d)
        pr, ds = [], []
        for side in range(2):
            cols = slice(side * TOK, (side + 1) * TOK)
            a = jnp.exp(masked(score[:, cols], lim_far[side]) - sth[side, h, 0:1, :])
            pr.append(a.astype(BF))
            ds.append((a * (dp[:, cols] - sth[side, h, 1:2, :])).astype(BF))
        dk = dk_acc[h] + nn(jnp.concatenate(ds, axis=1), q)
        dv = dv_acc[h] + nn(jnp.concatenate(pr, axis=1), d)
        dk_ref[0, :, c] = (dk * SCALE).astype(BF)
        dv_ref[0, :, c] = dv.astype(BF)
        return carry

    def y_round(s):
        for i in range(2):
            sh, ch = shard(s, 0), mine[i]
            wait_w(sh, ch)
            if s == 1:
                put(sh, ch, sy.at[4 + i], intra)
            put(sh, ch, sx.at[0, s, i], xr)
            put(sh, ch, sx.at[1, s, i], xl)
            put(sh, ch, ssib.at[s, i], sib)

    def x_round(s):
        for i in range(2):
            for side, dx in ((0, 3), (1, 1)):
                sh, ch = shard(s, dx), mine[i]
                wait_w(sh, ch)
                if i == side:
                    put(sh, ch, sx.at[side, s, 2], xr if side == 0 else xl)
                put(sh, ch, ssib.at[s, 2 + 2 * side + i], sib)

    def far_round(s):
        for i in range(2):
            sh, ch = shard(s, 2), mine[i]
            wait_w(sh, ch)
            put(sh, ch, ssib.at[s, 6 + i], sib)

    def sib_round(s):
        for dx in range(4):
            if s == 0 and dx == 0:
                continue
            for i in range(2):
                wait_w(shard(s, dx), theirs[i])

    past = wrap_hi.astype(jnp.int32)
    past_far = ((p // 2 == HALF_SEQ // 2) | wrap_lo).astype(jnp.int32)

    def run(fn, usual, other, which=past):
        lo = usual[0] * (1 - which) + other[0] * which
        hi = usual[1] * (1 - which) + other[1] * which
        lax.fori_loop(lo, hi, fn, 0)

    def halo_if(cond, i):
        @pl.when(cond)
        def _():
            wait_halo((i,))

    y_round(1)

    @pl.when(wrap_hi)
    def _():
        for i in range(3):
            to_relay(i).start()

    x_round(0)
    y_round(2)
    x_round(1)

    for copy in loads:
        copy.wait()
    halo_if(~wrap_hi, 0)
    run(early, (0, 4), (0, 0))
    y_round(3)
    far_round(0)
    pass_on(0)
    run(early, (4, 8), (0, 0))
    own_w.wait()
    sib_round(0)
    halo_if(~wrap_hi, 1)

    run(own_head, (0, 2), (0, 0))
    x_round(2)
    far_round(1)
    pass_on(1)
    sib_round(1)
    halo_if(wrap_hi, 0)
    run(early, (8, 8), (0, 8))
    run(own_head, (2, 4), (0, 0))
    x_round(3)
    far_round(2)
    pass_on(2)
    halo_if(~wrap_hi, 2)
    halo_if(wrap_hi, 1)

    @pl.when(wrap_hi)
    def _():
        pl.semaphore_wait(ready, 1)

    run(own_head, (4, 4), (0, 4))
    run(far_head, (0, 2), (0, 0), past_far)
    sib_round(2)
    run(own_head, (4, 6), (4, 6))
    far_round(3)
    halo_if(wrap_hi, 2)

    run(far_head, (2, 4), (0, 0), past_far)
    sib_round(3)
    run(own_head, (6, 8), (6, 8))

    run(far_head, (4, 8), (0, 8), past_far)

    for c in pending:
        c.wait_send()
    for part in halo_parts:
        halo(*part, 1 - core, sib).wait_send()

    @pl.when(has_z)
    def _():
        for part in halo_parts:
            halo(*part, core, zdev).wait_send()

    @pl.when(relays)
    def _():
        for i in range(3):
            relay(i).wait_send()

    def drain(h, carry):
        for copy in send_d(h, 1 - core, sib):
            copy.wait_send()

        @pl.when(has_z)
        def _():
            for copy in send_d(h, core, zdev):
                copy.wait_send()

        return carry

    lax.fori_loop(0, HEADS, drain, 0)


def body(queries, keys, values, d_out, w_out, pattern, valid):
    tok, width = queries.shape[1], queries.shape[2]
    vm = pl.BlockSpec(memory_space=pltpu.VMEM)
    sm = pl.BlockSpec(memory_space=pltpu.SMEM)
    hbm = pl.BlockSpec(memory_space=pltpu.HBM)
    out = jax.ShapeDtypeStruct((1, tok, width), BF)
    dma = pltpu.SemaphoreType.DMA
    return pl.pallas_call(
        kernel,
        out_shape=(out, out, out),
        in_specs=[sm, sm, hbm, hbm, hbm, hbm, hbm],
        out_specs=(vm, vm, vm),
        scratch_shapes=[
            pltpu.VMEM((3, tok, width), BF),
            pltpu.VMEM((3, tok, width), BF),
            pltpu.VMEM((3, tok, width), BF),
            pltpu.VMEM((tok, D), BF),
            pltpu.VMEM((16, 4, 16, D), BF),
            pltpu.VMEM((2, HEADS, tok, HD), BF),
            pltpu.VMEM((2, HEADS, 8, 128), F32),
            pltpu.VMEM((HEADS, tok, HD), BF),
            pltpu.VMEM((HEADS, 8, 128), F32),
            pltpu.VMEM((HEADS, 3 * tok, tok), F32),
            pltpu.VMEM((HEADS, tok, HD), F32),
            pltpu.VMEM((HEADS, tok, HD), F32),
            pltpu.VMEM((3, tok, width), BF),
            dma((16, 4)),
            dma((2, 4, 3)),
            dma((6,)),
            dma((4, 8)),
            dma((2, 3)),
            dma((2, 3)),
            dma((2, HEADS)),
            dma((2, HEADS)),
            dma((2, HEADS)),
            dma((2, HEADS)),
            dma,
            dma((4,)),
            pltpu.SemaphoreType.REGULAR,
            dma((3,)),
        ],
        compiler_params=pltpu.CompilerParams(
            collective_id=0, has_side_effects=True
        ),
        name="attention_backward",
    )(pattern.T, valid, queries, keys, values, d_out, w_out.reshape(4, 16, D))


def solution(mesh):
    spec = P("fsdp", "seq", None)
    in_specs = (spec, spec, spec, spec, P("fsdp", None), P(), P("fsdp", None))
    return jax.shard_map(
        body, mesh=mesh, in_specs=in_specs, out_specs=(spec, spec, spec), check_vma=False
    )
```

time: 62.1 us -> 55.8 us (0.90)
  Pallas kernels: 57.3 us -> 51.5 us
    pallas_call x1, Pallas kernels: 57.3 us -> 51.5 us  [body(): pl.pallas_call(kernel, out_shape=(out, out, out), in_specs=[sm, sm, hbm,...]
where the time goes in v2:
time: 55.8 us; the launch traced here: 55.6 us
  Pallas kernels  51.5 us (92%)
  local copies, waits for them, and re-layouts  3.46 us (6%)
  between operations  0.65 us (1%)
    pallas_call x1, Pallas kernels, body(): pl.pallas_call(kernel, out_shape=(out, out, out), in_specs=[sm, sm, hbm,...  51.5 us
    unnamed x7, local copies, waits for them, and re-layouts  3.46 us

profile of v2, /device:TPU:56, one launch (start us, length us, event | category | flops | bytes accessed | tf_op | source)
XLA Modules:
  0.0 55.6 jit_solution(18381651266000450401)
XLA Ops:
  0.6 51.5 %attention_backward.1 = (bf16[1,128,1024]{2,1,0:T(8,128)(2,1)}, bf16[1,128,1024]{2,1,0:T(8,128)(2,1)}, bf16[1,128,1024]{2,1,0:T(8,128)(2,1)}) custom-call(s32[4,48]{1,0:T(4,128)} %bitcast.3, s32[1,48]{1,0:T(1,128)} %val_ref.1, bf16[1,128,1024]{2,1,0:T(8,128)(2,1)} %q_hbm.1, bf16[1,128,1024]{2,1,0:T(8,128)(2,1)} %k_hbm.1, bf16[1,128,1024]{2,1,0:T(8,128)(2,1)} %v_hbm.1, ...), custom_call_target="tpu_custom_call" | custom-call | tf_op jit(solution)/shard_map/attention_backward/pallas_call | solution.py:430
  52.1 0.0 copy-start.1
  52.1 1.7 %copy.13 = bf16[1,128,1024]{2,1,0:T(8,128)(2,1)} copy(bf16[1,128,1024]{2,1,0:T(8,128)(2,1)} %get-tuple-element.6) | data formatting | bytes 524288
  53.8 0.0 copy-done.1
  53.8 0.0 copy-start
  53.8 0.7 %copy.14 = bf16[1,128,1024]{2,1,0:T(8,128)(2,1)} copy(bf16[1,128,1024]{2,1,0:T(8,128)(2,1)S(1)} %copy-done.1) | data formatting | bytes 524288
  54.5 0.3 copy-done
  54.9 0.7 %copy.15 = bf16[1,128,1024]{2,1,0:T(8,128)(2,1)} copy(bf16[1,128,1024]{2,1,0:T(8,128)(2,1)S(1)} %copy-done) | data formatting | bytes 524288
Async XLA Ops:
  52.1 1.7 %copy-start.1 = (bf16[1,128,1024]{2,1,0:T(8,128)(2,1)S(1)}, bf16[1,128,1024]{2,1,0:T(8,128)(2,1)}, u32[]{:S(2)}) copy-start(bf16[1,128,1024]{2,1,0:T(8,128)(2,1)} %get-tuple-element.7) | copy-start | bytes 786436
  53.8 1.0 %copy-start = (bf16[1,128,1024]{2,1,0:T(8,128)(2,1)S(1)}, bf16[1,128,1024]{2,1,0:T(8,128)(2,1)}, u32[]{:S(2)}) copy-start(bf16[1,128,1024]{2,1,0:T(8,128)(2,1)} %get-tuple-element.8) | copy-start | bytes 786436

commit v3 on v2

--- a/solution.py
+++ b/solution.py
@@ -324,12 +324,12 @@
             for i in range(2):
                 wait_w(shard(s, dx), theirs[i])
 
-    past = wrap_hi.astype(jnp.int32)
-    past_far = ((p // 2 == HALF_SEQ // 2) | wrap_lo).astype(jnp.int32)
-
-    def run(fn, usual, other, which=past):
-        lo = usual[0] * (1 - which) + other[0] * which
-        hi = usual[1] * (1 - which) + other[1] * which
+    last_z = ~(wrap_lo | wrap_hi) & ((p // 2) % (HALF_SEQ // 2) == HALF_SEQ // 2 - 1)
+    kinds = [kind.astype(jnp.int32) for kind in (~(wrap_lo | wrap_hi | last_z), wrap_hi, last_z, wrap_lo)]
+
+    def run(fn, *spans):
+        lo = sum(kind * span[0] for kind, span in zip(kinds, spans))
+        hi = sum(kind * span[1] for kind, span in zip(kinds, spans))
         lax.fori_loop(lo, hi, fn, 0)
 
     def halo_if(cond, i):
@@ -337,6 +337,8 @@
         def _():
             wait_halo((i,))
 
+    none = (0, 0)
+    leave = ((p // 2 == HALF_SEQ // 2) & ~wrap_hi).astype(jnp.int32)
     y_round(1)
 
     @pl.when(wrap_hi)
@@ -347,49 +349,48 @@
     x_round(0)
     y_round(2)
     x_round(1)
-
     for copy in loads:
         copy.wait()
-    halo_if(~wrap_hi, 0)
-    run(early, (0, 4), (0, 0))
+    usual = ~(wrap_hi | last_z | wrap_lo)
+    halo_if(usual, 0)
+    run(early, (0, 4), none, none, none)
+    pass_on(0)
     y_round(3)
     far_round(0)
-    pass_on(0)
-    run(early, (4, 8), (0, 0))
+    pass_on(1)
+    halo_if(wrap_lo, 0)
+    run(early, (4, 8), none, none, (0, 8))
     own_w.wait()
     sib_round(0)
-    halo_if(~wrap_hi, 1)
-
-    run(own_head, (0, 2), (0, 0))
+    halo_if(usual, 1)
+    run(own_head, (0, 2), none, none, none)
     x_round(2)
     far_round(1)
-    pass_on(1)
+    pass_on(2)
     sib_round(1)
     halo_if(wrap_hi, 0)
-    run(early, (8, 8), (0, 8))
-    run(own_head, (2, 4), (0, 0))
+    run(early, none, (0, 8), none, none)
     x_round(3)
     far_round(2)
-    pass_on(2)
-    halo_if(~wrap_hi, 2)
-    halo_if(wrap_hi, 1)
+    halo_if(usual, 2)
+    halo_if(wrap_hi | wrap_lo, 1)
 
     @pl.when(wrap_hi)
     def _():
         pl.semaphore_wait(ready, 1)
 
-    run(own_head, (4, 4), (0, 4))
-    run(far_head, (0, 2), (0, 0), past_far)
+    run(own_head, (2, 4), (0, 4), none, (0, 4))
     sib_round(2)
-    run(own_head, (4, 6), (4, 6))
     far_round(3)
-    halo_if(wrap_hi, 2)
-
-    run(far_head, (2, 4), (0, 0), past_far)
+    halo_if(last_z, 0)
+    halo_if(last_z, 1)
+    run(early, none, none, (0, 8), none)
+    run(own_head, (4, 6), (4, 6), (0, 6), (4, 6))
+    halo_if(~usual, 2)
+    run(far_head, (0, 4 * (1 - leave)), none, none, none)
     sib_round(3)
-    run(own_head, (6, 8), (6, 8))
-
-    run(far_head, (4, 8), (0, 8), past_far)
+    run(own_head, (6, 8), (6, 8), (6, 8), (6, 8))
+    run(far_head, (4 * (1 - leave), 8), (0, 8), (0, 8), (0, 8))
 
     for c in pending:
         c.wait_send()
@@ -418,6 +419,26 @@
         return carry
 
     lax.fori_loop(0, HEADS, drain, 0)
+
+
+def write_out(dq, dk, dv, dq_out, dk_out, dv_out, held, sem_in, sem_out):
+    half = TOK // 2
+    steps = []
+    for i, (src, dst) in enumerate(((dq, dq_out), (dk, dk_out), (dv, dv_out))):
+        for j in range(2):
+            rows = pl.ds(j * half, half)
+            n = 2 * i + j
+            steps.append((
+                pltpu.make_async_copy(src.at[0, rows], held.at[i, rows], sem_in.at[n]),
+                pltpu.make_async_copy(held.at[i, rows], dst.at[0, rows], sem_out.at[n]),
+            ))
+    for first, _ in steps:
+        first.start()
+    for first, second in steps:
+        first.wait()
+        second.start()
+    for _, second in steps:
+        second.wait()
 
 
 def body(queries, keys, values, d_out, w_out, pattern, valid):
@@ -427,7 +448,7 @@
     hbm = pl.BlockSpec(memory_space=pltpu.HBM)
     out = jax.ShapeDtypeStruct((1, tok, width), BF)
     dma = pltpu.SemaphoreType.DMA
-    return pl.pallas_call(
+    grads = pl.pallas_call(
         kernel,
         out_shape=(out, out, out),
         in_specs=[sm, sm, hbm, hbm, hbm, hbm, hbm],
@@ -466,6 +487,15 @@
         ),
         name="attention_backward",
     )(pattern.T, valid, queries, keys, values, d_out, w_out.reshape(4, 16, D))
+    hb = pl.BlockSpec(memory_space=pl.ANY)
+    return pl.pallas_call(
+        write_out,
+        out_shape=(out, out, out),
+        in_specs=[hb, hb, hb],
+        out_specs=(hb, hb, hb),
+        scratch_shapes=[pltpu.VMEM((3, tok, width), BF), dma((6,)), dma((6,))],
+        name="write_out",
+    )(*grads)
 
 
 def solution(mesh):

time: 55.8 us -> 51.2 us (0.918)
  local copies, waits for them, and re-layouts: 3.46 us -> 0 us
  Pallas kernels: 51.5 us -> 49.9 us
    pallas_call x1, Pallas kernels: 51.5 us -> 47.9 us  [body(): pl.pallas_call(kernel, out_shape=(out, out, out), in_specs=[sm, sm, hbm,...]
    unnamed x7 -> x0, local copies, waits for them, and re-layouts: 3.46 us -> none
    pallas_call x0 -> x1, Pallas kernels: none -> 1.97 us  [body(): pl.pallas_call(write_out, out_shape=(out, out, out), in_specs=[hb, hb, hb...]
where the time goes in v3:
time: 51.2 us; the launch traced here: 50.5 us
  Pallas kernels  49.9 us (97%)
  between operations  0.64 us (1%)
    pallas_call x1, Pallas kernels, body(): pl.pallas_call(kernel, out_shape=(out, out, out), in_specs=[sm, sm, hbm,...  47.9 us
    pallas_call x1, Pallas kernels, body(): pl.pallas_call(write_out, out_shape=(out, out, out), in_specs=[hb, hb, hb...  1.97 us

profile of v3, /device:TPU:56, one launch (start us, length us, event | category | flops | bytes accessed | tf_op | source)
XLA Modules:
  0.0 50.5 jit_solution(1684600073653727430)
XLA Ops:
  0.6 47.9 %attention_backward.1 = (bf16[1,128,1024]{2,1,0:T(8,128)(2,1)}, bf16[1,128,1024]{2,1,0:T(8,128)(2,1)}, bf16[1,128,1024]{2,1,0:T(8,128)(2,1)}) custom-call(s32[4,48]{1,0:T(4,128)} %bitcast.3, s32[1,48]{1,0:T(1,128)} %val_ref.1, bf16[1,128,1024]{2,1,0:T(8,128)(2,1)} %q_hbm.1, bf16[1,128,1024]{2,1,0:T(8,128)(2,1)} %k_hbm.1, bf16[1,128,1024]{2,1,0:T(8,128)(2,1)} %v_hbm.1, ...), custom_call_target="tpu_custom_call" | custom-call | tf_op jit(solution)/shard_map/attention_backward/pallas_call | solution.py:451
  48.6 2.0 %write_out.1 = (bf16[1,128,1024]{2,1,0:T(8,128)(2,1)}, bf16[1,128,1024]{2,1,0:T(8,128)(2,1)}, bf16[1,128,1024]{2,1,0:T(8,128)(2,1)}) custom-call(bf16[1,128,1024]{2,1,0:T(8,128)(2,1)} %get-tuple-element.6.dq, bf16[1,128,1024]{2,1,0:T(8,128)(2,1)} %get-tuple-element.7.dk, bf16[1,128,1024]{2,1,0:T(8,128)(2,1)} %get-tuple-element.8.dv), custom_call_target="tpu_custom_call" | custom-call | tf_op jit(solution)/shard_map/write_out/pallas_call | solution.py:491

commit v4 on v3

--- a/solution.py
+++ b/solution.py
@@ -124,6 +124,15 @@
         c.start()
         pending.append(c)
 
+    def pair(sh, row, ssem):
+        rows = wf.at[sh, pl.ds(row, 2)]
+        return rcopy(rows, rows, ssem, wr.at[sh, row], sib)
+
+    def put_pair(sh, ssem):
+        c = pair(sh, 2 * core, ssem)
+        c.start()
+        pending.append(c)
+
     def wait_w(sh, ch):
         rcopy(wf.at[sh, ch], wf.at[sh, ch], lsem, wr.at[sh, ch], sib).wait_recv()
 
@@ -131,7 +140,6 @@
         return ((k_y + sgn * ORDER[s] + 4) % 4) * 4 + (x + dx) % 4
 
     mine = (2 * core, 2 * core + 1)
-    theirs = (2 - 2 * core, 3 - 2 * core)
 
     for i in range(2):
         put_own(mine[i], sy.at[i], inter)
@@ -300,7 +308,7 @@
                 put(sh, ch, sy.at[4 + i], intra)
             put(sh, ch, sx.at[0, s, i], xr)
             put(sh, ch, sx.at[1, s, i], xl)
-            put(sh, ch, ssib.at[s, i], sib)
+        put_pair(shard(s, 0), ssib.at[s, 0])
 
     def x_round(s):
         for i in range(2):
@@ -309,20 +317,19 @@
                 wait_w(sh, ch)
                 if i == side:
                     put(sh, ch, sx.at[side, s, 2], xr if side == 0 else xl)
-                put(sh, ch, ssib.at[s, 2 + 2 * side + i], sib)
+        put_pair(shard(s, 3), ssib.at[s, 1])
+        put_pair(shard(s, 1), ssib.at[s, 2])
 
     def far_round(s):
         for i in range(2):
-            sh, ch = shard(s, 2), mine[i]
-            wait_w(sh, ch)
-            put(sh, ch, ssib.at[s, 6 + i], sib)
+            wait_w(shard(s, 2), mine[i])
+        put_pair(shard(s, 2), ssib.at[s, 3])
 
     def sib_round(s):
         for dx in range(4):
             if s == 0 and dx == 0:
                 continue
-            for i in range(2):
-                wait_w(shard(s, dx), theirs[i])
+            pair(shard(s, dx), 2 - 2 * core, lsem).wait_recv()
 
     last_z = ~(wrap_lo | wrap_hi) & ((p // 2) % (HALF_SEQ // 2) == HALF_SEQ // 2 - 1)
     kinds = [kind.astype(jnp.int32) for kind in (~(wrap_lo | wrap_hi | last_z), wrap_hi, last_z, wrap_lo)]
@@ -470,7 +477,7 @@
             dma((16, 4)),
             dma((2, 4, 3)),
             dma((6,)),
-            dma((4, 8)),
+            dma((4, 4)),
             dma((2, 3)),
             dma((2, 3)),
             dma((2, HEADS)),

time: 51.2 us -> 51 us (level)
  no operation moved by 1% of the time
where the time goes in v4:
time: 51 us; the launch traced here: 50.3 us
  Pallas kernels  49.7 us (97%)
  between operations  0.64 us (1%)
    pallas_call x1, Pallas kernels, body(): pl.pallas_call(kernel, out_shape=(out, out, out), in_specs=[sm, sm, hbm,...  47.7 us
    pallas_call x1, Pallas kernels, body(): pl.pallas_call(write_out, out_shape=(out, out, out), in_specs=[hb, hb, hb...  1.97 us

profile of v4, /device:TPU:56, one launch (start us, length us, event | category | flops | bytes accessed | tf_op | source)
XLA Modules:
  0.0 50.3 jit_solution(12113906600615492844)
XLA Ops:
  0.6 47.7 %attention_backward.1 = (bf16[1,128,1024]{2,1,0:T(8,128)(2,1)}, bf16[1,128,1024]{2,1,0:T(8,128)(2,1)}, bf16[1,128,1024]{2,1,0:T(8,128)(2,1)}) custom-call(s32[4,48]{1,0:T(4,128)} %bitcast.3, s32[1,48]{1,0:T(1,128)} %val_ref.1, bf16[1,128,1024]{2,1,0:T(8,128)(2,1)} %q_hbm.1, bf16[1,128,1024]{2,1,0:T(8,128)(2,1)} %k_hbm.1, bf16[1,128,1024]{2,1,0:T(8,128)(2,1)} %v_hbm.1, ...), custom_call_target="tpu_custom_call" | custom-call | tf_op jit(solution)/shard_map/attention_backward/pallas_call | solution.py:458
  48.4 2.0 %write_out.1 = (bf16[1,128,1024]{2,1,0:T(8,128)(2,1)}, bf16[1,128,1024]{2,1,0:T(8,128)(2,1)}, bf16[1,128,1024]{2,1,0:T(8,128)(2,1)}) custom-call(bf16[1,128,1024]{2,1,0:T(8,128)(2,1)} %get-tuple-element.6.dq, bf16[1,128,1024]{2,1,0:T(8,128)(2,1)} %get-tuple-element.7.dk, bf16[1,128,1024]{2,1,0:T(8,128)(2,1)} %get-tuple-element.8.dv), custom_call_target="tpu_custom_call" | custom-call | tf_op jit(solution)/shard_map/write_out/pallas_call | solution.py:498

commit v5 on v4

--- a/solution.py
+++ b/solution.py
@@ -429,12 +429,12 @@
 
 
 def write_out(dq, dk, dv, dq_out, dk_out, dv_out, held, sem_in, sem_out):
-    half = TOK // 2
+    part = TOK // 4
     steps = []
     for i, (src, dst) in enumerate(((dq, dq_out), (dk, dk_out), (dv, dv_out))):
-        for j in range(2):
-            rows = pl.ds(j * half, half)
-            n = 2 * i + j
+        for j in range(4):
+            rows = pl.ds(j * part, part)
+            n = 4 * i + j
             steps.append((
                 pltpu.make_async_copy(src.at[0, rows], held.at[i, rows], sem_in.at[n]),
                 pltpu.make_async_copy(held.at[i, rows], dst.at[0, rows], sem_out.at[n]),
@@ -500,7 +500,7 @@
         out_shape=(out, out, out),
         in_specs=[hb, hb, hb],
         out_specs=(hb, hb, hb),
-        scratch_shapes=[pltpu.VMEM((3, tok, width), BF), dma((6,)), dma((6,))],
+        scratch_shapes=[pltpu.VMEM((3, tok, width), BF), dma((12,)), dma((12,))],
         name="write_out",
     )(*grads)
 

time: 51 us -> 51.1 us (level)
  no operation moved by 1% of the time
where the time goes in v5:
time: 51.1 us; the launch traced here: 50.4 us
  Pallas kernels  49.7 us (97%)
  between operations  0.64 us (1%)
    pallas_call x1, Pallas kernels, body(): pl.pallas_call(kernel, out_shape=(out, out, out), in_specs=[sm, sm, hbm,...  47.7 us
    pallas_call x1, Pallas kernels, body(): pl.pallas_call(write_out, out_shape=(out, out, out), in_specs=[hb, hb, hb...  2 us

profile of v5, /device:TPU:56, one launch (start us, length us, event | category | flops | bytes accessed | tf_op | source)
XLA Modules:
  0.0 50.4 jit_solution(15437515332075653392)
XLA Ops:
  0.6 47.7 %attention_backward.1 = (bf16[1,128,1024]{2,1,0:T(8,128)(2,1)}, bf16[1,128,1024]{2,1,0:T(8,128)(2,1)}, bf16[1,128,1024]{2,1,0:T(8,128)(2,1)}) custom-call(s32[4,48]{1,0:T(4,128)} %bitcast.3, s32[1,48]{1,0:T(1,128)} %val_ref.1, bf16[1,128,1024]{2,1,0:T(8,128)(2,1)} %q_hbm.1, bf16[1,128,1024]{2,1,0:T(8,128)(2,1)} %k_hbm.1, bf16[1,128,1024]{2,1,0:T(8,128)(2,1)} %v_hbm.1, ...), custom_call_target="tpu_custom_call" | custom-call | tf_op jit(solution)/shard_map/attention_backward/pallas_call | solution.py:458
  48.4 2.0 %write_out.1 = (bf16[1,128,1024]{2,1,0:T(8,128)(2,1)}, bf16[1,128,1024]{2,1,0:T(8,128)(2,1)}, bf16[1,128,1024]{2,1,0:T(8,128)(2,1)}) custom-call(bf16[1,128,1024]{2,1,0:T(8,128)(2,1)} %get-tuple-element.6.dq, bf16[1,128,1024]{2,1,0:T(8,128)(2,1)} %get-tuple-element.7.dk, bf16[1,128,1024]{2,1,0:T(8,128)(2,1)} %get-tuple-element.8.dv), custom_call_target="tpu_custom_call" | custom-call | tf_op jit(solution)/shard_map/write_out/pallas_call | solution.py:498
